TPU v7x, 32 devices: a whole 2x2x4 slice. The times are simulated.
32 devices in a mesh: groups: 1, samp: 4 (over x, core), var: 8 (over z, y).
Axes of the slice: x: 2, y: 2, z: 4, core: 2. Of those that a mesh axis runs over, the one named last changes fastest.
Arguments:
- expression: bfloat16 [4096, 5120], P(('groups', 'samp'), 'var'), may hold values from -6 to 6
- genotypes: bfloat16 [4096, 1536], P(('groups', 'samp'), 'var'), may hold values from 0 to 2
- covariates: bfloat16 [4096, 64], P(('groups', 'samp')), may hold values from -6 to 6
- distance_bins: int32 [24, 5120], P('groups', ('var', 'samp')), may hold values from 0 to 15
- gene_folds: int32 [5120], P(('groups', 'var', 'samp')), may hold values from 0 to 4
- fold_weights: float32 [5, 16], replicated, may hold values from 0.25 to 4
Outputs:
- weighted_stats: float32 [5120, 1536], P(('groups', 'var', 'samp'))
Inputs may be any that keep to these rules, and one draw needn't show every extreme that they name: `distance_bins`: bins index rows of fold_weights' second dimension. `gene_folds`: folds index rows of fold_weights.
All inputs are finite; a program needn't handle non-finite values.
Results may differ from a plain program's by a relative error of at most 0.0047.
Values may be sent and summed in bfloat16 or wider, within the bound.
A program may use at most 64 MiB of HBM per device.

v0:
```python
import jax
import jax.numpy as jnp
from jax import lax
from jax.sharding import PartitionSpec as P

COVS = 64
VARS = 1536
VTILE = 64
NBINS = 16
FOLDS = 5
VTILES = 24


def solve_fit(data, design, factor, cross):
    beta = jax.scipy.linalg.cho_solve((factor, True), cross)
    fitted = jnp.dot(design.astype(jnp.float32), beta, precision=lax.Precision.HIGHEST)
    return (beta, data.astype(jnp.float32) - fitted)


def shards(expression, genotypes, covariates, distance_bins, gene_folds, fold_weights):
    sample_rows = expression.shape[0]
    samples = sample_rows * lax.axis_size("samp")
    design = jnp.concatenate([jnp.ones((sample_rows, 1), jnp.bfloat16), covariates], axis=1)
    source = lax.all_gather(genotypes, "var", axis=1, tiled=True)
    gram = jnp.dot(design.T, design, preferred_element_type=jnp.float32)
    expr_cross = jnp.dot(design.T, expression, preferred_element_type=jnp.float32)
    geno_cross = jnp.dot(design.T, source, preferred_element_type=jnp.float32)
    partial_sums = (gram, expr_cross, geno_cross)
    summed = lax.psum((partial_sums[0], partial_sums[1], partial_sums[2]), "samp")
    gram, expr_cross, geno_cross = (summed[0], summed[1], summed[2])
    factor = jnp.linalg.cholesky(gram)
    expr_beta, expr_resid = solve_fit(expression, design, factor, expr_cross)
    geno_beta, geno_resid = solve_fit(source, design, factor, geno_cross)
    expr_norm, geno_norm = lax.psum(
        (jnp.sum(expr_resid * expr_resid, axis=0), jnp.sum(geno_resid * geno_resid, axis=0)), "samp"
    )
    expr_unit = (expr_resid * lax.rsqrt(expr_norm + 1e-06)).astype(jnp.bfloat16)
    geno_unit = (geno_resid * lax.rsqrt(geno_norm + 1e-06)).astype(jnp.bfloat16)
    terms = lax.dot_general(
        expr_unit, geno_unit, (((0,), (0,)), ((), ())), preferred_element_type=jnp.float32
    )
    corr = lax.psum_scatter(terms, "samp", scatter_dimension=0, tiled=True)
    local_genes = corr.shape[0]
    fold_onehot = (gene_folds[:, None] == jnp.arange(FOLDS)[None, :]).astype(jnp.float32)
    row_weights = jnp.dot(fold_onehot, fold_weights, precision=lax.Precision.HIGHEST)
    bin_match = distance_bins.T[:, :, None] == jnp.arange(NBINS)[None, None, :]
    tile_weight = jnp.sum(jnp.where(bin_match, row_weights[:, None, :], 0.0), axis=2)
    dof = jnp.float32(samples - COVS - 2)
    stats = dof * corr * corr
    weighted = stats.reshape(local_genes, VTILES, VTILE) * tile_weight[:, :, None]
    return weighted.reshape(local_genes, VARS)


def solution(mesh):
    return jax.shard_map(
        shards,
        mesh=mesh,
        in_specs=(
            P(("groups", "samp"), "var"),
            P(("groups", "samp"), "var"),
            P(("groups", "samp"), None),
            P("groups", ("var", "samp")),
            P(("groups", "var", "samp")),
            P(),
        ),
        out_specs=P(("groups", "var", "samp"), None),
        check_vma=False,
    )
```

profile of v0, /device:TPU:0, one launch (start us, length us, event | category | flops | bytes accessed | tf_op | source)
XLA Modules:
  0.0 191.9 jit_solution(71797673533566679)
XLA Ops:
  6.5 0.7 all-gather.2.cloned.1.call-update
  7.3 0.0 all-reduce.5.cloned.1.call-start
  7.3 1.2 fusion.11
  8.5 13.2 %psum.35 = f32[65,65]{0,1:T(8,128)S(1)} all-reduce(f32[65,65]{0,1:T(8,128)S(1)} %fusion.11), channel_id=1, replica_groups=mesh['groups'=1,'samp'=4,'var'=8] {'samp'}, use_global_device_ids=true, to_apply=%region_0.0 | all-reduce | flops 4225 | bytes 33800 | tf_op jit(solution)/shard_map/psum | solution.py:29
  21.7 0.1 copy.23
  21.8 5.9 %cholesky.16 = f32[65,65]{1,0:T(8,128)S(1)} custom-call(f32[65,65]{1,0:T(8,128)S(1)} %fusion.24), custom_call_target="Cholesky" | custom-call | tf_op jit(solution)/shard_map/jit(cholesky)/cholesky | solution.py:31
  27.8 2.4 %fusion.9 = f32[65,640]{1,0:T(8,128)} fusion(bf16[1024,640]{1,0:T(8,128)(2,1)} %param.6, bf16[1024,64]{0,1:T(8,128)(2,1)} %param.8), kind=kOutput, calls=%fused_computation.18 | convolution fusion | flops 85196800 | bytes 1608192 | tf_op jit(solution)/shard_map/dot_general | solution.py:26
  30.2 42.2 %all-gather.2.cloned.1.call-done = bf16[1024,1536]{0,1:T(8,128)(2,1)} async-done(((bf16[1024,192]{0,1:T(8,128)(2,1)}), bf16[1024,1536]{0,1:T(8,128)(2,1)}) %all-gather.2.cloned.1.call-update) | async-done | bytes 3145744 | tf_op jit(solution)/shard_map/all_gather | solution.py:24
  72.4 4.0 %fusion.5 = f32[65,1536]{1,0:T(8,128)} fusion(bf16[1024,1536]{0,1:T(8,128)(2,1)} %all-gather.2.cloned.1.call-done, bf16[1024,64]{0,1:T(8,128)(2,1)} %param.8), kind=kOutput, calls=%fused_computation.14 | convolution fusion | flops 204472320 | bytes 3676160 | tf_op jit(solution)/shard_map/dot_general | solution.py:27
  76.3 0.0 reduce-scatter.2.cloned.1.call-start
  76.4 0.7 compare_reduce_fusion
  77.1 0.6 fusion.15
  77.7 5.0 %custom-call.16 = f32[1,65,65]{1,2,0:T(8,128)S(1)} custom-call(f32[1,65,65]{2,1,0:T(8,128)S(1)} %fusion.15), custom_call_target="InvertDiagBlocksLowerTriangular" | custom-call | tf_op jit(solution)/shard_map/jit(_cho_solve)/triangular_solve | solution.py:15
  82.7 3.0 %copy.24 = bf16[1024,1536]{1,0:T(8,128)(2,1)} copy(bf16[1024,1536]{0,1:T(8,128)(2,1)S(1)} %copy-done.1) | data formatting | bytes 6291456 | tf_op jit(solution)/shard_map/all_gather | solution.py:24
  85.7 23.3 %all-reduce.5.cloned.1.call-done = (f32[65,1536]{1,0:T(8,128)}, f32[65,640]{1,0:T(8,128)}) async-done(((f32[65,1536]{1,0:T(8,128)}, f32[65,640]{1,0:T(8,128)}), (f32[65,1536]{1,0:T(8,128)}, f32[65,640]{1,0:T(8,128)})) %all-reduce.5.cloned.1.call-update) | async-done | bytes 565776 | tf_op jit(solution)/shard_map/psum | solution.py:29
  108.9 1.6 fusion.18
  110.5 0.5 fusion.16
  111.1 1.4 fusion.22
  112.5 0.3 fusion.20
  112.9 3.0 %multiply_reduce_fusion.1 = (f32[640]{0:T(1024)S(1)}, f32[1024,640]{1,0:T(8,128)}) fusion(bf16[1024,640]{1,0:T(8,128)(2,1)S(1)} %copy-done.3, f32[65,640]{1,0:T(8,128)S(1)} %fusion.20, bf16[1024,64]{0,1:T(8,128)(2,1)S(1)} %copy-done.4), kind=kOutput, calls=%fused_computation.6 | convolution fusion | flops 513801600 | bytes 4232192 | tf_op jit(solution)/shard_map/dot_general | solution.py:16
  115.8 5.1 %multiply_reduce_fusion = (f32[1536]{0:T(1024)S(1)}, f32[1024,1536]{1,0:T(8,128)}) fusion(f32[65,1536]{1,0:T(8,128)S(1)} %fusion.16, bf16[1024,64]{0,1:T(8,128)(2,1)S(1)} %copy-done.4, bf16[1024,1536]{1,0:T(8,128)(2,1)S(1)} %copy-done.2), kind=kOutput, calls=%fused_computation.1 | convolution fusion | flops 1233123840 | bytes 9973760 | tf_op jit(solution)/shard_map/dot_general | solution.py:16
  120.9 10.3 %all-reduce.1 = (f32[1536]{0:T(1024)S(1)}, f32[640]{0:T(1024)S(1)}) all-reduce(f32[1536]{0:T(1024)S(1)} %get-tuple-element.9, f32[640]{0:T(1024)S(1)} %get-tuple-element.11), channel_id=1, replica_groups=mesh['groups'=1,'samp'=4,'var'=8] {'samp'}, use_global_device_ids=true, to_apply=%region_8.9 | all-reduce | flops 2176 | bytes 17408 | tf_op jit(solution)/shard_map/psum | solution.py:34
  131.2 7.9 %fusion = f32[640,1536]{1,0:T(8,128)} fusion(f32[1024,1536]{1,0:T(8,128)} %get-tuple-element.10, f32[1536]{0:T(1024)S(1)} %add_rsqrt_fusion, f32[1024,640]{1,0:T(8,128)} %get-tuple-element.12, bf16[1024,640]{1,0:T(8,128)(2,1)S(1)} %copy-done.3, f32[640]{0:T(1024)S(1)} %add_rsqrt_fusion.1), kind=kOutput, calls=%fused_computation.3 | convolution fusion | flops 2019033088 | bytes 14164480 | tf_op jit(solution)/shard_map/dot_general | solution.py:39
  139.1 0.6 copy-done.6
  139.8 0.2 fusion.13
  140.0 0.0 copy-done.5
  140.0 0.1 select_reduce_fusion
  140.1 0.1 copy.25
  140.2 0.6 mul.51
  140.8 0.5 mul.52
  141.3 41.7 %reduce-scatter.2.cloned.1.call-done = f32[160,1536]{1,0:T(8,128)} async-done(((f32[640,1536]{1,0:T(8,128)}), f32[160,1536]{1,0:T(8,128)}) %reduce-scatter.2.cloned.1.call-update) | async-done | bytes 983056 | tf_op jit(solution)/shard_map/reduce_scatter | solution.py:42
  183.0 2.3 %fusion.3 = f32[160,1536]{1,0:T(8,128)} fusion(f32[160,1536]{1,0:T(8,128)S(1)} %mul.52, f32[160,1536]{1,0:T(8,128)} %reduce-scatter.2.cloned.1.call-done), kind=kLoop, calls=%fused_computation.10 | loop fusion | flops 737280 | bytes 2949120 | tf_op jit(solution)/shard_map/mul | solution.py:50
  (19 shorter events, 0.1 us)
Async XLA Ops:
  6.5 132.6 %copy-start = (f32[5,16]{1,0:T(8,128)S(1)}, f32[5,16]{1,0:T(8,128)}, u32[]{:S(2)}) copy-start(f32[5,16]{1,0:T(8,128)} %param.11) | copy-start | bytes 964
  6.5 65.8 %all-gather.2.cloned.1.call-start = ((), (), s32[]{:S(2)}) async-start(), calls=%async_computation.1 | async-start | bytes 3538944 | tf_op jit(solution)/shard_map/all_gather | solution.py:24
  7.3 101.7 %all-reduce.5.cloned.1.call-start = ((), (), s32[]{:S(2)}) async-start(), calls=%async_computation.3 | async-start | bytes 1253376 | tf_op jit(solution)/shard_map/psum | solution.py:29
  72.4 10.3 %copy-start.1 = (bf16[1024,1536]{0,1:T(8,128)(2,1)S(1)}, bf16[1024,1536]{0,1:T(8,128)(2,1)}, u32[]{:S(2)}) copy-start(bf16[1024,1536]{0,1:T(8,128)(2,1)} %all-gather.2.cloned.1.call-done) | copy-start | bytes 9437188
  76.3 106.7 %reduce-scatter.2.cloned.1.call-start = ((), (), s32[]{:S(2)}) async-start(), calls=%async_computation.2 | async-start | bytes 4915200 | tf_op jit(solution)/shard_map/reduce_scatter | solution.py:42
  85.7 27.2 %copy-start.3 = (bf16[1024,640]{1,0:T(8,128)(2,1)S(1)}, bf16[1024,640]{1,0:T(8,128)(2,1)}, u32[]{:S(2)}) copy-start(bf16[1024,640]{1,0:T(8,128)(2,1)} %param.6) | copy-start | bytes 3932164
  85.7 27.2 %copy-start.4 = (bf16[1024,64]{0,1:T(8,128)(2,1)S(1)}, bf16[1024,64]{0,1:T(8,128)(2,1)}, u32[]{:S(2)}) copy-start(bf16[1024,64]{0,1:T(8,128)(2,1)} %param.8) | copy-start | bytes 393220
  111.0 4.8 %copy-start.2 = (bf16[1024,1536]{1,0:T(8,128)(2,1)S(1)}, bf16[1024,1536]{1,0:T(8,128)(2,1)}, u32[]{:S(2)}) copy-start(bf16[1024,1536]{1,0:T(8,128)(2,1)} %copy.24) | copy-start | bytes 9437188
  139.1 0.7 copy-start.6
  139.1 0.9 copy-start.5
Sparse Core Ops, SparseCore 0:
  9.5 62.8 all-gather.1
  76.5 32.4 all-reduce.4
  139.2 43.7 reduce-scatter.1
where the time goes:
time: 192 us
  waiting for transfers between devices  108 us (56%)
  matrix products  27.5 us (14%)
  blocking collectives  23.5 us (12%)
  other arithmetic  14.7 us (8%)
  between operations  13.2 us (7%)
  local copies, waits for them, and re-layouts  4.89 us (3%)
    all_gather x1, waiting for transfers between devices, shards(): source = lax.all_gather(genotypes, 'var', axis=1, tiled=True)  42.2 us
    reduce_scatter x1, waiting for transfers between devices, shards(): corr = lax.psum_scatter(terms, 'samp', scatter_dimension=0, tiled=True)  41.7 us
    psum x1, waiting for transfers between devices, shards(): lax.psum((partial_sums[0], partial_sums[1], partial_sums[2]), 'samp')  23.3 us
    psum x1, blocking collectives, shards(): lax.psum((partial_sums[0], partial_sums[1], partial_sums[2]), 'samp')  13.2 us
    psum x1, blocking collectives, shards(): lax.psum((jnp.sum(expr_resid * expr_resid, axis=0), jnp.sum(geno_resid *...  10.3 us
    dot_general x2, matrix products, solve_fit(): jnp.dot(design.astype(jnp.float32), beta, precision=lax.Precision.HIGHEST)  8.05 us
    dot_general x1, matrix products, shards(): lax.dot_general(expr_unit, geno_unit, (((0,), (0,)), ((), ())), preferred...  7.86 us
    another operation x3, other arithmetic, shards(): factor = jnp.linalg.cholesky(gram)  6.64 us
  transfers between devices with their start and end apart: 3, of which 3 were waited for; matrix products, arithmetic and copies ran while one was open for 11% of the time, Pallas kernels for 0%

commit v1 on v0

--- a/solution.py
+++ b/solution.py
@@ -21,7 +21,9 @@
     sample_rows = expression.shape[0]
     samples = sample_rows * lax.axis_size("samp")
     design = jnp.concatenate([jnp.ones((sample_rows, 1), jnp.bfloat16), covariates], axis=1)
-    source = lax.all_gather(genotypes, "var", axis=1, tiled=True)
+    source = jnp.concatenate(
+        lax.all_to_all(jnp.stack([genotypes] * lax.axis_size("var")), "var", 0, 0), axis=1
+    )
     gram = jnp.dot(design.T, design, preferred_element_type=jnp.float32)
     expr_cross = jnp.dot(design.T, expression, preferred_element_type=jnp.float32)
     geno_cross = jnp.dot(design.T, source, preferred_element_type=jnp.float32)

time: 192 us -> 206 us (1.073)
  starting transfers between devices: 0.08 us -> 7.52 us
  waiting for transfers between devices: 108 us -> 115 us
  matrix products: 27.5 us -> 24.4 us
  local copies, waits for them, and re-layouts: 4.89 us -> 7.96 us
    all_to_all x0 -> x1, waiting for transfers between devices: none -> 50.4 us  [shards(): lax.all_to_all(jnp.stack([genotypes] * lax.axis_size('var')), 'var', 0, 0)]
    all_gather x1 -> x0, waiting for transfers between devices: 42.2 us -> none  [shards(): source = lax.all_gather(genotypes, 'var', axis=1, tiled=True)]
    all_to_all x0 -> x1, starting transfers between devices: none -> 7.44 us  [shards(): lax.all_to_all(jnp.stack([genotypes] * lax.axis_size('var')), 'var', 0, 0)]
    another operation x0 -> x1, local copies, waits for them, and re-layouts: none -> 3.07 us  [shards(): jnp.stack([genotypes] * lax.axis_size('var'))]
    all_gather x1 -> x0, local copies, waits for them, and re-layouts: 2.97 us -> none  [shards(): source = lax.all_gather(genotypes, 'var', axis=1, tiled=True)]
    reshape x0 -> x1, local copies, waits for them, and re-layouts: none -> 2.97 us  [shards(): jnp.concatenate(lax.all_to_all(jnp.stack([genotypes] * lax.axis_size('var...]
    dot_general x1, matrix products: 3.95 us -> 1.85 us  [shards(): geno_cross = jnp.dot(design.T, source, preferred_element_type=jnp.float32)]
  transfers between devices with their start and end apart: 3 -> 3, of which waited for: 3 -> 3; matrix products, arithmetic and copies ran while one was open for 11% -> 9% of each run, Pallas kernels for 0% -> 0%
where the time goes in v1:
time: 206 us
  waiting for transfers between devices  115 us (56%)
  matrix products  24.4 us (12%)
  blocking collectives  22 us (11%)
  other arithmetic  14.9 us (7%)
  between operations  13.5 us (7%)
  local copies, waits for them, and re-layouts  7.96 us (4%)
  starting transfers between devices  7.52 us (4%)
    all_to_all x1, waiting for transfers between devices, shards(): lax.all_to_all(jnp.stack([genotypes] * lax.axis_size('var')), 'var', 0, 0)  50.4 us
    reduce_scatter x1, waiting for transfers between devices, shards(): corr = lax.psum_scatter(terms, 'samp', scatter_dimension=0, tiled=True)  41.4 us
    psum x1, waiting for transfers between devices, shards(): lax.psum((partial_sums[0], partial_sums[1], partial_sums[2]), 'samp')  23.6 us
    psum x1, blocking collectives, shards(): lax.psum((partial_sums[0], partial_sums[1], partial_sums[2]), 'samp')  11.7 us
    psum x1, blocking collectives, shards(): lax.psum((jnp.sum(expr_resid * expr_resid, axis=0), jnp.sum(geno_resid *...  10.3 us
    dot_general x2, matrix products, solve_fit(): jnp.dot(design.astype(jnp.float32), beta, precision=lax.Precision.HIGHEST)  8.07 us
    dot_general x1, matrix products, shards(): lax.dot_general(expr_unit, geno_unit, (((0,), (0,)), ((), ())), preferred...  7.86 us
    all_to_all x1, starting transfers between devices, shards(): lax.all_to_all(jnp.stack([genotypes] * lax.axis_size('var')), 'var', 0, 0)  7.44 us
  transfers between devices with their start and end apart: 3, of which 3 were waited for; matrix products, arithmetic and copies ran while one was open for 9% of the time, Pallas kernels for 0%

profile of v1, /device:TPU:0, one launch (start us, length us, event | category | flops | bytes accessed | tf_op | source)
XLA Modules:
  0.0 205.6 jit_solution(16160813606714416573)
XLA Ops:
  6.5 3.1 %stack.2 = bf16[8,1024,192]{1,2,0:T(8,128)(2,1)} broadcast(bf16[1024,192]{0,1:T(8,128)(2,1)} %param.7), dimensions={1,2} | broadcast | bytes 3538944 | tf_op jit(solution)/shard_map/stack | solution.py:25
  9.6 7.4 %all-to-all-start = ((bf16[8,1024,192]{1,2,0:T(8,128)(2,1)}), bf16[8,1024,192]{1,2,0:T(8,128)(2,1)S(1)}, u32[]{:S(2)}, u32[]{:S(2)}) async-start(bf16[8,1024,192]{1,2,0:T(8,128)(2,1)} %stack.2), calls=%async_computation | async-start | bytes 6291456 | tf_op jit(solution)/shard_map/all_to_all | solution.py:25
  17.1 0.0 all-reduce.5.cloned.1.call-start
  17.1 0.2 fusion.11
  17.3 11.7 %psum.35 = f32[65,65]{0,1:T(8,128)S(1)} all-reduce(f32[65,65]{0,1:T(8,128)S(1)} %fusion.11), channel_id=1, replica_groups=mesh['groups'=1,'samp'=4,'var'=8] {'samp'}, use_global_device_ids=true, to_apply=%region_0.0 | all-reduce | flops 4225 | bytes 33800 | tf_op jit(solution)/shard_map/psum | solution.py:31
  29.0 0.1 copy.18
  29.1 5.9 %cholesky.16 = f32[65,65]{1,0:T(8,128)S(1)} custom-call(f32[65,65]{1,0:T(8,128)S(1)} %fusion.24), custom_call_target="Cholesky" | custom-call | tf_op jit(solution)/shard_map/jit(cholesky)/cholesky | solution.py:33
  35.1 2.3 %fusion.9 = f32[65,640]{1,0:T(8,128)} fusion(bf16[1024,640]{1,0:T(8,128)(2,1)} %param.6, bf16[1024,64]{0,1:T(8,128)(2,1)S(1)} %copy-done.3), kind=kOutput, calls=%fused_computation.18 | convolution fusion | flops 85196800 | bytes 1608192 | tf_op jit(solution)/shard_map/dot_general | solution.py:28
  37.4 50.4 %all-to-all-done = bf16[8,1024,192]{1,2,0:T(8,128)(2,1)S(1)} async-done(((bf16[8,1024,192]{1,2,0:T(8,128)(2,1)}), bf16[8,1024,192]{1,2,0:T(8,128)(2,1)S(1)}, u32[]{:S(2)}, u32[]{:S(2)}) %all-to-all-start) | async-done | bytes 3145760 | tf_op jit(solution)/shard_map/all_to_all | solution.py:25
  87.8 1.9 fusion.5
  89.6 0.0 reduce-scatter.2.cloned.1.call-start
  89.7 0.7 compare_reduce_fusion
  90.4 0.7 fusion.15
  91.1 5.0 %custom-call.16 = f32[1,65,65]{1,2,0:T(8,128)S(1)} custom-call(f32[1,65,65]{2,1,0:T(8,128)S(1)} %fusion.15), custom_call_target="InvertDiagBlocksLowerTriangular" | custom-call | tf_op jit(solution)/shard_map/jit(_cho_solve)/triangular_solve | solution.py:15
  96.1 3.0 %copy.19 = bf16[1024,1536]{1,0:T(8,128)(2,1)} copy(bf16[1024,1536]{0,1:T(8,128)(2,1)S(1)} %bitcast.29) | data formatting | bytes 6291456 | tf_op jit(solution)/shard_map/reshape | solution.py:24
  99.1 23.6 %all-reduce.5.cloned.1.call-done = (f32[65,1536]{1,0:T(8,128)}, f32[65,640]{1,0:T(8,128)}) async-done(((f32[65,1536]{1,0:T(8,128)}, f32[65,640]{1,0:T(8,128)}), (f32[65,1536]{1,0:T(8,128)}, f32[65,640]{1,0:T(8,128)})) %all-reduce.5.cloned.1.call-update) | async-done | bytes 565776 | tf_op jit(solution)/shard_map/psum | solution.py:31
  122.7 1.6 fusion.18
  124.3 0.5 fusion.16
  124.8 1.4 fusion.22
  126.3 0.3 fusion.20
  126.6 3.0 %multiply_reduce_fusion.1 = (f32[640]{0:T(1024)S(1)}, f32[1024,640]{1,0:T(8,128)}) fusion(bf16[1024,640]{1,0:T(8,128)(2,1)S(1)} %copy-done.2, f32[65,640]{1,0:T(8,128)S(1)} %fusion.20, bf16[1024,64]{0,1:T(8,128)(2,1)S(1)} %copy-done.3), kind=kOutput, calls=%fused_computation.6 | convolution fusion | flops 513801600 | bytes 4232192 | tf_op jit(solution)/shard_map/dot_general | solution.py:16
  129.6 5.1 %multiply_reduce_fusion = (f32[1536]{0:T(1024)S(1)}, f32[1024,1536]{1,0:T(8,128)}) fusion(f32[65,1536]{1,0:T(8,128)S(1)} %fusion.16, bf16[1024,64]{0,1:T(8,128)(2,1)S(1)} %copy-done.3, bf16[1024,1536]{1,0:T(8,128)(2,1)S(1)} %copy-done.1), kind=kOutput, calls=%fused_computation.1 | convolution fusion | flops 1233123840 | bytes 9973760 | tf_op jit(solution)/shard_map/dot_general | solution.py:16
  134.7 10.3 %all-reduce.1 = (f32[1536]{0:T(1024)S(1)}, f32[640]{0:T(1024)S(1)}) all-reduce(f32[1536]{0:T(1024)S(1)} %get-tuple-element.9, f32[640]{0:T(1024)S(1)} %get-tuple-element.11), channel_id=1, replica_groups=mesh['groups'=1,'samp'=4,'var'=8] {'samp'}, use_global_device_ids=true, to_apply=%region_8.9 | all-reduce | flops 2176 | bytes 17408 | tf_op jit(solution)/shard_map/psum | solution.py:36
  145.0 7.9 %fusion = f32[640,1536]{1,0:T(8,128)} fusion(f32[1024,1536]{1,0:T(8,128)} %get-tuple-element.10, f32[1536]{0:T(1024)S(1)} %add_rsqrt_fusion, f32[1024,640]{1,0:T(8,128)} %get-tuple-element.12, bf16[1024,640]{1,0:T(8,128)(2,1)S(1)} %copy-done.2, f32[640]{0:T(1024)S(1)} %add_rsqrt_fusion.1), kind=kOutput, calls=%fused_computation.3 | convolution fusion | flops 2019033088 | bytes 14164480 | tf_op jit(solution)/shard_map/dot_general | solution.py:41
  152.9 0.6 copy-done.5
  153.5 0.2 fusion.13
  153.8 0.1 select_reduce_fusion
  153.9 0.1 copy.20
  154.0 0.6 mul.51
  154.6 0.5 mul.52
  155.1 41.4 %reduce-scatter.2.cloned.1.call-done = f32[160,1536]{1,0:T(8,128)} async-done(((f32[640,1536]{1,0:T(8,128)}), f32[160,1536]{1,0:T(8,128)}) %reduce-scatter.2.cloned.1.call-update) | async-done | bytes 983056 | tf_op jit(solution)/shard_map/reduce_scatter | solution.py:44
  196.4 2.3 %fusion.3 = f32[160,1536]{1,0:T(8,128)} fusion(f32[160,1536]{1,0:T(8,128)S(1)} %mul.52, f32[160,1536]{1,0:T(8,128)} %reduce-scatter.2.cloned.1.call-done), kind=kLoop, calls=%fused_computation.10 | loop fusion | flops 737280 | bytes 2949120 | tf_op jit(solution)/shard_map/mul | solution.py:52
  (17 shorter events, 0.1 us)
Async XLA Ops:
  6.5 146.4 %copy-start = (f32[5,16]{1,0:T(8,128)S(1)}, f32[5,16]{1,0:T(8,128)}, u32[]{:S(2)}) copy-start(f32[5,16]{1,0:T(8,128)} %param.11) | copy-start | bytes 964
  9.6 7.5 %copy-start.3 = (bf16[1024,64]{0,1:T(8,128)(2,1)S(1)}, bf16[1024,64]{0,1:T(8,128)(2,1)}, u32[]{:S(2)}) copy-start(bf16[1024,64]{0,1:T(8,128)(2,1)} %param.8) | copy-start | bytes 393220
  9.6 78.2 %all-to-all-start = ((bf16[8,1024,192]{1,2,0:T(8,128)(2,1)}), bf16[8,1024,192]{1,2,0:T(8,128)(2,1)S(1)}, u32[]{:S(2)}, u32[]{:S(2)}) async-start(bf16[8,1024,192]{1,2,0:T(8,128)(2,1)} %stack.2), calls=%async_computation | async-start | bytes 6291456 | tf_op jit(solution)/shard_map/all_to_all | solution.py:25
  17.1 105.7 %all-reduce.5.cloned.1.call-start = ((), (), s32[]{:S(2)}) async-start(), calls=%async_computation.3 | async-start | bytes 1253376 | tf_op jit(solution)/shard_map/psum | solution.py:31
  89.6 106.8 %reduce-scatter.2.cloned.1.call-start = ((), (), s32[]{:S(2)}) async-start(), calls=%async_computation.2 | async-start | bytes 4915200 | tf_op jit(solution)/shard_map/reduce_scatter | solution.py:44
  99.1 27.5 %copy-start.2 = (bf16[1024,640]{1,0:T(8,128)(2,1)S(1)}, bf16[1024,640]{1,0:T(8,128)(2,1)}, u32[]{:S(2)}) copy-start(bf16[1024,640]{1,0:T(8,128)(2,1)} %param.6) | copy-start | bytes 3932164
  124.8 4.8 %copy-start.1 = (bf16[1024,1536]{1,0:T(8,128)(2,1)S(1)}, bf16[1024,1536]{1,0:T(8,128)(2,1)}, u32[]{:S(2)}) copy-start(bf16[1024,1536]{1,0:T(8,128)(2,1)} %copy.19) | copy-start | bytes 9437188
  152.9 0.7 copy-start.5
  152.9 0.9 copy-start.4
Sparse Core Ops, SparseCore 0:
  89.8 32.9 all-reduce.4
  153.0 43.3 reduce-scatter.1
